TPU v7x, 256 devices: a whole 4x4x8 slice. The times are simulated.
256 devices in a mesh: row: 8 (over x, z_hi), col: 32 (over y, z_lo, core).
Axes of the slice: x: 4, y: 4, z: 8 (z_hi: 2, z_lo: 4; z = z_hi * 4 + z_lo), core: 2. Of those that a mesh axis runs over, the one named last changes fastest.
Arguments:
- matrix: float32 [16384, 16384], P('row', 'col'), may hold values from -6 to 6, as said below
- vectors: float32 [2, 16384, 128], P(None, ('row', 'col')), may hold values from -0.16 to 0.16
- tfactor: float32 [2, 128, 128], replicated, may hold values from -0.5 to 0.5
Outputs:
- updated: float32 [16384, 16384], P('row', 'col')
Inputs may be any that keep to these rules, and one draw needn't show every extreme that they name: matrix is symmetric: matrix[i, j] equals matrix[j, i].
All inputs are finite; a program needn't handle non-finite values.
Results may differ from a plain program's by a relative error of at most 0.00012.
Values sent between devices are 32-bit elements; how exact they have to be, the bound alone decides.
A program may use at most 64 MiB of HBM per device.

v0:
```python
import jax
import jax.numpy as jnp
from jax import lax
from jax.sharding import PartitionSpec as P

highest = lax.Precision.HIGHEST


def spread(block, axis, source):
    block = jnp.where(lax.axis_index(axis) == source, block, jnp.zeros_like(block))
    return lax.psum(block, axis)


def mat_product(left, right):
    return jnp.dot(left, right, precision=highest, preferred_element_type=jnp.float32)


def body(matrix, vectors, tfactor):
    rows_here, cols_here = matrix.shape
    panels = vectors.shape[0]
    own_count = vectors.shape[1]
    row_total = lax.axis_size("row")
    col_total = lax.axis_size("col")
    row_index = lax.axis_index("row")
    col_index = lax.axis_index("col")
    owner_row = col_index * row_total // col_total
    offset = col_index * cols_here - owner_row * rows_here
    v_rows = lax.all_gather(vectors, "col", axis=1, tiled=True)
    v_local = lax.dynamic_slice_in_dim(v_rows, offset, cols_here, 1)
    v_cols = spread(v_local, "row", owner_row)
    current = matrix
    for panel_index in range(panels):
        vector_i = v_rows[panel_index]
        vector_j = v_cols[panel_index]
        own_rows = vectors[panel_index]
        factor = jnp.triu(tfactor[panel_index])

        def partial_rows(begin_row, span_rows, current=current, vector_j=vector_j):
            return mat_product(current, vector_j)

        summed = lax.psum_scatter(
            partial_rows(jnp.int32(0), own_count * lax.axis_size("col")),
            "col",
            scatter_dimension=0,
            tiled=True,
        )
        ymatrix = mat_product(summed, factor)
        gram_matrix = lax.psum(mat_product(own_rows.T, ymatrix), ("row", "col"))
        w_own = ymatrix - 0.5 * mat_product(own_rows, mat_product(factor.T, gram_matrix))
        w_all = lax.all_gather(w_own, ("row", "col"), axis=0, tiled=True)
        w_i = lax.dynamic_slice_in_dim(w_all, row_index * rows_here, rows_here, 0)
        w_j = lax.dynamic_slice_in_dim(w_all, col_index * cols_here, cols_here, 0)
        current = current - mat_product(vector_i, w_j.T) - mat_product(w_i, vector_j.T)
    return current


def solution(mesh):
    return jax.shard_map(
        body,
        mesh=mesh,
        in_specs=(P("row", "col"), P(None, ("row", "col"), None), P()),
        out_specs=P("row", "col"),
        check_vma=False,
    )
```

profile of v0, /device:TPU:32, one launch (start us, length us, event | category | flops | bytes accessed | tf_op | source)
XLA Modules:
  0.0 1845.8 jit_solution(2119604143348090658)
XLA Ops:
  7.3 64.0 %all-gather.4.cloned.1.call-done = f32[2,2048,128]{2,1,0:T(8,128)} async-done(((f32[2,64,128]{2,1,0:T(8,128)}), f32[2,2048,128]{2,1,0:T(8,128)}) %all-gather.4.cloned.1.call-update) | async-done | bytes 2097168 | tf_op jit(solution)/shard_map/all_gather | solution.py:28
  71.3 1.9 dynamic-slice_select_fusion
  73.2 110.7 %all-reduce.4.cloned.1.call-done = f32[2,512,128]{2,1,0:T(8,128)} async-done(((f32[2,512,128]{2,1,0:T(8,128)}), f32[2,512,128]{2,1,0:T(8,128)}) %all-reduce.4.cloned.1.call-update) | async-done | bytes 524304 | tf_op jit(solution)/shard_map/psum | solution.py:11
  184.0 6.7 convolution_bitcast_fusion
  190.7 1.3 copy.14
  192.1 136.8 %reduce-scatter.7.cloned.1.call-done = f32[64,128]{1,0:T(8,128)} async-done(((f32[2048,128]{1,0:T(8,128)}), f32[64,128]{1,0:T(8,128)}) %reduce-scatter.7.cloned.1.call-update) | async-done | bytes 32784
  328.9 1.0 fusion.14
  330.0 0.9 convolution_bitcast_fusion.2
  331.0 245.8 %all-reduce.6.cloned.1.call-done = f32[128,128]{0,1:T(8,128)} async-done(((f32[128,128]{0,1:T(8,128)}), f32[128,128]{0,1:T(8,128)}) %all-reduce.6.cloned.1.call-update) | async-done | bytes 65552 | tf_op jit(solution)/shard_map/psum | solution.py:48
  576.7 1.2 fusion.13
  578.8 5.5 copy.8
  584.3 412.1 %all-gather.6.cloned.1.call-done = f32[16384,128]{1,0:T(8,128)} async-done(((f32[64,128]{1,0:T(8,128)}), f32[16384,128]{1,0:T(8,128)}) %all-gather.6.cloned.1.call-update) | async-done | bytes 8388624 | tf_op jit(solution)/shard_map/all_gather | solution.py:50
  996.5 4.9 fusion.8
  1001.4 4.9 fusion.1
  1006.3 2.0 copy-done
  1008.3 8.1 fusion.12
  1016.5 138.2 %reduce-scatter.5.cloned.1.call-done = f32[64,128]{1,0:T(8,128)} async-done(((f32[2048,128]{1,0:T(8,128)}), f32[64,128]{1,0:T(8,128)}) %reduce-scatter.5.cloned.1.call-update) | async-done | bytes 32784 | tf_op jit(solution)/shard_map/reduce_scatter | solution.py:41
  1154.7 1.0 fusion.16
  1156.7 245.8 %all-reduce.8.cloned.1.call-done = f32[128,128]{0,1:T(8,128)} async-done(((f32[128,128]{0,1:T(8,128)}), f32[128,128]{0,1:T(8,128)}) %all-reduce.8.cloned.1.call-update) | async-done | bytes 65552 | tf_op jit(solution)/shard_map/psum | solution.py:48
  1402.5 1.2 fusion.15
  1404.5 417.7 %all-gather.8.cloned.1.call-done = f32[16384,128]{1,0:T(8,128)} async-done(((f32[64,128]{1,0:T(8,128)}), f32[16384,128]{1,0:T(8,128)}) %all-gather.8.cloned.1.call-update) | async-done | bytes 8388624 | tf_op jit(solution)/shard_map/all_gather | solution.py:50
  1822.2 4.9 fusion.6
  1827.1 6.5 fusion
  1833.6 5.3 copy.11
  (33 shorter events, 3.7 us)
Async XLA Ops:
  6.5 64.7 %all-gather.4.cloned.1.call-start = ((), (), s32[]{:S(2)}) async-start(), calls=%async_computation.2 | async-start | bytes 2162688 | tf_op jit(solution)/shard_map/all_gather | solution.py:28
  7.3 176.7 %all-reduce.4.cloned.1.call-start = ((), (), s32[]{:S(2)}) async-start(), calls=%async_computation.3 | async-start | bytes 1048576 | tf_op jit(solution)/shard_map/psum | solution.py:11
  73.2 255.8 %copy-start.6 = (f32[2,128,128]{2,1,0:T(8,128)S(1)}, f32[2,128,128]{2,1,0:T(8,128)}, u32[]{:S(2)}) copy-start(f32[2,128,128]{2,1,0:T(8,128)} %param.5) | copy-start | bytes 393220
  73.2 256.8 %copy-start.5 = (f32[2,64,128]{2,1,0:T(8,128)S(1)}, f32[2,64,128]{2,1,0:T(8,128)}, u32[]{:S(2)}) copy-start(f32[2,64,128]{2,1,0:T(8,128)} %param.4) | copy-start | bytes 196612
  73.2 255.7 %reduce-scatter.7.cloned.1.call-start = ((), (), s32[]{:S(2)}) async-start(), calls=%async_computation.9 | async-start | bytes 1081344
  192.1 384.7 %all-reduce.6.cloned.1.call-start = ((), (), s32[]{:S(2)}) async-start(), calls=%async_computation.4 | async-start | bytes 131072 | tf_op jit(solution)/shard_map/psum | solution.py:48
  330.9 665.6 %all-gather.6.cloned.1.call-start = ((), (), s32[]{:S(2)}) async-start(), calls=%async_computation.5 | async-start | bytes 8421376 | tf_op jit(solution)/shard_map/all_gather | solution.py:50
  578.8 576.0 %reduce-scatter.5.cloned.1.call-start = ((), (), s32[]{:S(2)}) async-start(), calls=%async_computation.6 | async-start | bytes 1081344 | tf_op jit(solution)/shard_map/reduce_scatter | solution.py:41
  578.8 417.6 %copy-start.4 = (f32[2,512,128]{2,1,0:T(8,128)S(1)}, f32[2,512,128]{2,1,0:T(8,128)}, u32[]{:S(2)}) copy-start(f32[2,512,128]{2,1,0:T(8,128)} %all-reduce.4.cloned.1.call-done) | copy-start | bytes 1572868
  578.8 422.5 %copy-start.3 = (f32[2,2048,128]{2,1,0:T(8,128)S(1)}, f32[2,2048,128]{2,1,0:T(8,128)}, u32[]{:S(2)}) copy-start(f32[2,2048,128]{2,1,0:T(8,128)} %all-gather.4.cloned.1.call-done) | copy-start | bytes 6291460
  996.5 4.9 copy-start.2
  1006.3 2.0 copy-start
  1016.4 386.1 %all-reduce.8.cloned.1.call-start = ((), (), s32[]{:S(2)}) async-start(), calls=%async_computation.7 | async-start | bytes 131072 | tf_op jit(solution)/shard_map/psum | solution.py:48
  1156.7 665.5 %all-gather.8.cloned.1.call-start = ((), (), s32[]{:S(2)}) async-start(), calls=%async_computation.8 | async-start | bytes 8421376 | tf_op jit(solution)/shard_map/all_gather | solution.py:50
  1822.2 4.9 copy-start.1
Sparse Core Ops, SparseCore 0:
  9.2 62.0 all-gather.3
  73.9 110.0 all-reduce.3
  192.2 136.7 reduce-scatter.6
  334.3 242.4 all-reduce.5
  578.9 417.5 all-gather.5
  1016.6 138.1 reduce-scatter.4
  1160.2 242.2 all-reduce.7
  1404.7 417.5 all-gather.7
where the time goes:
time: 1850 us
  waiting for transfers between devices  1770 us (96%)
  matrix products  43.8 us (2%)
    all_gather x2, waiting for transfers between devices, body(): w_all = lax.all_gather(w_own, ('row', 'col'), axis=0, tiled=True)  830 us
    psum x2, waiting for transfers between devices, body(): gram_matrix = lax.psum(mat_product(own_rows.T, ymatrix), ('row', 'col'))  492 us
    reduce_scatter x1, waiting for transfers between devices, body(): lax.psum_scatter(partial_rows(jnp.int32(0), own_count * lax.axis_size('co...  138 us
    unnamed x9, waiting for transfers between devices  138 us
    psum x1, waiting for transfers between devices, spread(): return lax.psum(block, axis)  111 us
    all_gather x1, waiting for transfers between devices, body(): v_rows = lax.all_gather(vectors, 'col', axis=1, tiled=True)  64 us
    dot_general x14, matrix products, mat_product(): jnp.dot(left, right, precision=highest, preferred_element_type=jnp.float32)  43.8 us
  transfers between devices with their start and end apart: 8, of which 8 were waited for; matrix products, arithmetic and copies ran while one was open for 0% of the time, Pallas kernels for 0%

commit v1 on v0

--- a/solution.py
+++ b/solution.py
@@ -45,7 +45,9 @@
             tiled=True,
         )
         ymatrix = mat_product(summed, factor)
-        gram_matrix = lax.psum(mat_product(own_rows.T, ymatrix), ("row", "col"))
+        gram_matrix = jnp.sum(
+            lax.all_gather(mat_product(own_rows.T, ymatrix), ("row", "col")), axis=0
+        )
         w_own = ymatrix - 0.5 * mat_product(own_rows, mat_product(factor.T, gram_matrix))
         w_all = lax.all_gather(w_own, ("row", "col"), axis=0, tiled=True)
         w_i = lax.dynamic_slice_in_dim(w_all, row_index * rows_here, rows_here, 0)

time: 1850 us -> 2270 us (1.23)
  waiting for transfers between devices: 1770 us -> 2150 us
  local copies, waits for them, and re-layouts: 14.2 us -> 42.4 us
    all_gather x0 -> x2, waiting for transfers between devices: none -> 867 us  [body(): lax.all_gather(mat_product(own_rows.T, ymatrix), ('row', 'col'))]
    psum x2 -> x0, waiting for transfers between devices: 492 us -> none  [body(): gram_matrix = lax.psum(mat_product(own_rows.T, ymatrix), ('row', 'col'))]
    unnamed x16 -> x18, local copies, waits for them, and re-layouts: 8.84 us -> 37 us
where the time goes in v1:
time: 2270 us
  waiting for transfers between devices  2150 us (95%)
  local copies, waits for them, and re-layouts  42.4 us (2%)
  matrix products  42.2 us (2%)
    all_gather x2, waiting for transfers between devices, body(): lax.all_gather(mat_product(own_rows.T, ymatrix), ('row', 'col'))  867 us
    all_gather x2, waiting for transfers between devices, body(): w_all = lax.all_gather(w_own, ('row', 'col'), axis=0, tiled=True)  832 us
    reduce_scatter x1, waiting for transfers between devices, body(): lax.psum_scatter(partial_rows(jnp.int32(0), own_count * lax.axis_size('co...  138 us
    unnamed x9, waiting for transfers between devices  138 us
    psum x1, waiting for transfers between devices, spread(): return lax.psum(block, axis)  111 us
    all_gather x1, waiting for transfers between devices, body(): v_rows = lax.all_gather(vectors, 'col', axis=1, tiled=True)  64 us
  transfers between devices with their start and end apart: 8, of which 8 were waited for; matrix products, arithmetic and copies ran while one was open for 0% of the time, Pallas kernels for 0%

profile of v1, /device:TPU:32, one launch (start us, length us, event | category | flops | bytes accessed | tf_op | source)
XLA Modules:
  0.0 2266.3 jit_solution(6753853804692090868)
XLA Ops:
  7.3 64.0 %all-gather.8.cloned.1.call-done = f32[2,2048,128]{2,1,0:T(8,128)} async-done(((f32[2,64,128]{2,1,0:T(8,128)}), f32[2,2048,128]{2,1,0:T(8,128)}) %all-gather.8.cloned.1.call-update) | async-done | bytes 2097168 | tf_op jit(solution)/shard_map/all_gather | solution.py:28
  71.3 1.9 dynamic-slice_select_fusion
  73.2 110.7 %all-reduce.2.cloned.1.call-done = f32[2,512,128]{2,1,0:T(8,128)} async-done(((f32[2,512,128]{2,1,0:T(8,128)}), f32[2,512,128]{2,1,0:T(8,128)}) %all-reduce.2.cloned.1.call-update) | async-done | bytes 524304 | tf_op jit(solution)/shard_map/psum | solution.py:11
  184.0 6.7 convolution_bitcast_fusion
  190.7 1.3 copy.14
  192.1 136.8 %reduce-scatter.7.cloned.1.call-done = f32[64,128]{1,0:T(8,128)} async-done(((f32[2048,128]{1,0:T(8,128)}), f32[64,128]{1,0:T(8,128)}) %reduce-scatter.7.cloned.1.call-update) | async-done | bytes 32784
  328.9 1.0 fusion.14
  331.0 433.8 %all-gather.14.cloned.1.call-done = f32[32768,128]{0,1:T(8,128)} async-done(((f32[128,128]{0,1:T(8,128)}), f32[32768,128]{0,1:T(8,128)}) %all-gather.14.cloned.1.call-update) | async-done | bytes 16777232 | tf_op jit(solution)/shard_map/all_gather | solution.py:49
  764.8 14.1 copy.16
  778.9 8.0 bitcast_reduce_fusion.1
  788.2 5.5 copy.8
  793.7 413.1 %all-gather.10.cloned.1.call-done = f32[16384,128]{1,0:T(8,128)} async-done(((f32[64,128]{1,0:T(8,128)}), f32[16384,128]{1,0:T(8,128)}) %all-gather.10.cloned.1.call-update) | async-done | bytes 8388624 | tf_op jit(solution)/shard_map/all_gather | solution.py:52
  1206.8 4.9 fusion.8
  1211.7 4.9 fusion.1
  1216.6 2.0 copy-done
  1218.6 8.1 fusion.12
  1226.8 138.3 %reduce-scatter.5.cloned.1.call-done = f32[64,128]{1,0:T(8,128)} async-done(((f32[2048,128]{1,0:T(8,128)}), f32[64,128]{1,0:T(8,128)}) %reduce-scatter.5.cloned.1.call-update) | async-done | bytes 32784 | tf_op jit(solution)/shard_map/reduce_scatter | solution.py:41
  1367.1 433.6 %all-gather.16.cloned.1.call-done = f32[32768,128]{0,1:T(8,128)} async-done(((f32[128,128]{0,1:T(8,128)}), f32[32768,128]{0,1:T(8,128)}) %all-gather.16.cloned.1.call-update) | async-done | bytes 16777232 | tf_op jit(solution)/shard_map/all_gather | solution.py:49
  1800.7 14.1 copy.17
  1814.8 8.0 bitcast_reduce_fusion
  1824.1 418.6 %all-gather.12.cloned.1.call-done = f32[16384,128]{1,0:T(8,128)} async-done(((f32[64,128]{1,0:T(8,128)}), f32[16384,128]{1,0:T(8,128)}) %all-gather.12.cloned.1.call-update) | async-done | bytes 8388624 | tf_op jit(solution)/shard_map/all_gather | solution.py:52
  2242.7 4.9 fusion.6
  2247.6 6.5 fusion
  2254.1 5.3 copy.11
  (37 shorter events, 6.3 us)
Async XLA Ops:
  6.5 64.7 %all-gather.8.cloned.1.call-start = ((), (), s32[]{:S(2)}) async-start(), calls=%async_computation.2 | async-start | bytes 2162688 | tf_op jit(solution)/shard_map/all_gather | solution.py:28
  7.3 176.7 %all-reduce.2.cloned.1.call-start = ((), (), s32[]{:S(2)}) async-start(), calls=%async_computation.3 | async-start | bytes 1048576 | tf_op jit(solution)/shard_map/psum | solution.py:11
  73.2 255.8 %copy-start.6 = (f32[2,128,128]{2,1,0:T(8,128)S(1)}, f32[2,128,128]{2,1,0:T(8,128)}, u32[]{:S(2)}) copy-start(f32[2,128,128]{2,1,0:T(8,128)} %param.5) | copy-start | bytes 393220
  73.2 256.8 %copy-start.5 = (f32[2,64,128]{2,1,0:T(8,128)S(1)}, f32[2,64,128]{2,1,0:T(8,128)}, u32[]{:S(2)}) copy-start(f32[2,64,128]{2,1,0:T(8,128)} %param.4) | copy-start | bytes 196612
  73.2 255.7 %reduce-scatter.7.cloned.1.call-start = ((), (), s32[]{:S(2)}) async-start(), calls=%async_computation.9 | async-start | bytes 1081344
  192.1 572.7 %all-gather.14.cloned.1.call-start = ((), (), s32[]{:S(2)}) async-start(), calls=%async_computation.7 | async-start | bytes 16842752 | tf_op jit(solution)/shard_map/all_gather | solution.py:49
  330.9 875.8 %all-gather.10.cloned.1.call-start = ((), (), s32[]{:S(2)}) async-start(), calls=%async_computation.4 | async-start | bytes 8421376 | tf_op jit(solution)/shard_map/all_gather | solution.py:52
  788.1 577.0 %reduce-scatter.5.cloned.1.call-start = ((), (), s32[]{:S(2)}) async-start(), calls=%async_computation.5 | async-start | bytes 1081344 | tf_op jit(solution)/shard_map/reduce_scatter | solution.py:41
  788.2 418.6 %copy-start.4 = (f32[2,512,128]{2,1,0:T(8,128)S(1)}, f32[2,512,128]{2,1,0:T(8,128)}, u32[]{:S(2)}) copy-start(f32[2,512,128]{2,1,0:T(8,128)} %all-reduce.2.cloned.1.call-done) | copy-start | bytes 1572868
  788.2 423.5 %copy-start.3 = (f32[2,2048,128]{2,1,0:T(8,128)S(1)}, f32[2,2048,128]{2,1,0:T(8,128)}, u32[]{:S(2)}) copy-start(f32[2,2048,128]{2,1,0:T(8,128)} %all-gather.8.cloned.1.call-done) | copy-start | bytes 6291460
  1206.8 4.9 copy-start.2
  1216.6 2.0 copy-start
  1226.7 574.0 %all-gather.16.cloned.1.call-start = ((), (), s32[]{:S(2)}) async-start(), calls=%async_computation.8 | async-start | bytes 16842752 | tf_op jit(solution)/shard_map/all_gather | solution.py:49
  1367.1 875.6 %all-gather.12.cloned.1.call-start = ((), (), s32[]{:S(2)}) async-start(), calls=%async_computation.6 | async-start | bytes 8421376 | tf_op jit(solution)/shard_map/all_gather | solution.py:52
  2242.7 4.9 copy-start.1
Sparse Core Ops, SparseCore 0:
  9.2 62.0 all-gather.7
  73.9 110.0 all-reduce.1
  192.2 136.7 reduce-scatter.6
  331.0 433.7 all-gather.13
  788.2 418.4 all-gather.9
  1226.9 138.2 reduce-scatter.4
  1367.2 433.4 all-gather.15
  1824.2 418.4 all-gather.11
